TPU v7x, 32 devices: a whole 2x2x4 slice. The times are simulated.
32 devices in a mesh: grp: 2 (over y), user: 4 (over z), tm: 4 (over x, core).
Axes of the slice: x: 2, y: 2, z: 4, core: 2. Of those that a mesh axis runs over, the one named last changes fastest.
Arguments:
- history: bfloat16 [8, 1024, 512], P(('grp', 'user'), 'tm'), parts along dimension 0, may hold values from -6 to 6
- z_weight: bfloat16 [512, 1024], replicated, may hold values from -0.25 to 0.25
- xbc_weight: bfloat16 [512, 1280], replicated, may hold values from -0.25 to 0.25
- dt_weight: bfloat16 [512, 16], replicated, may hold values from -0.125 to 0.125
- dt_bias: float32 [16], replicated, may hold values from -1 to 0.5
- a_log: float32 [16], replicated
- conv_weight: float32 [4, 1280], replicated, may hold values from -3 to 3
- conv_bias: float32 [1280], replicated, may hold values from -3 to 3
- d_skip: float32 [16], replicated, may hold values from 0.5 to 1.5
- norm_gain: float32 [1024], replicated, may hold values from 0.1 to 1.9
- out_weight: bfloat16 [1024, 512], replicated, may hold values from -0.1875 to 0.1875
- label_pos: int32 [8, 2048], P(('grp', 'user'), 'tm'), parts along dimension 0, may hold values from 0 to 1023, as said below
- label_count: int32 [8, 4], P(('grp', 'user'), 'tm'), parts along dimension 0, may hold values from 1 to 511, as said below
- label_value: int32 [8, 2048], P(('grp', 'user'), 'tm'), parts along dimension 0, may hold values 0 or 1
- item_feat: bfloat16 [8, 2048, 512], P(('grp', 'user'), 'tm'), parts along dimension 0, may hold values from -6 to 6
- first_weight: bfloat16 [1024, 1024], replicated, may hold values from -0.1875 to 0.1875
- second_weight: bfloat16 [1024], replicated, may hold values from -0.1875 to 0.1875
Outputs:
- encoded: bfloat16 [8, 1024, 512], P(('grp', 'user'), 'tm'), parts along dimension 0
- row_logit: float32 [8, 2048], P(('grp', 'user'), 'tm'), parts along dimension 0
- grad_first: float32 [2048, 1024], P('grp'), parts along dimension 0
- grad_second: float32 [2048], P('grp'), parts along dimension 0
There are 2 independent parts, one for each index of `grp`. A program takes and returns all parts, laid end to end along the dimension named above; an argument that names none is the same for every part. Nothing has to cross between parts.
Inputs may be any that keep to these rules, and one draw needn't show every extreme that they name: `label_pos`: positions in slots k * 512 to (k + 1) * 512 - 1 of a user lie in events k * 256 to (k + 1) * 256 - 1. label_count[u, k] slots are used in block k of user u's slots, and they are the block's first ones; the counts of blocks 2 * k and 2 * k + 1 of a user sum to 512.
All inputs are finite; a program needn't handle non-finite values. No bound on the sum of `label_value` on one device may be relied on, other than what follows from the above.
Results may differ from a plain program's by a relative error of at most 0.015.
Values may be sent and summed in bfloat16 or wider, within the bound.
No kernel may reach another device: no remote copies, remote signals or barrier semaphores. Data moves between devices by JAX's collectives and lax.ppermute only.
A program may use at most 64 MiB of HBM per device.

v0:
```python
import jax
import jax.numpy as jnp
from jax import lax
from jax.sharding import PartitionSpec as P

BLOCK = 256


def passed_along(shard, axis, by):
    peers = lax.axis_size(axis)
    pairs = [(i, i + by) for i in range(peers) if 0 <= i + by < peers]
    return lax.ppermute(shard, axis, pairs)


def silu_grad(values):
    sig = jax.nn.sigmoid(values)
    return sig * (1.0 + values * (1.0 - sig))


def ranker(rank_rows, target, live_mask, first_weight, second_weight):
    pre_act = jnp.dot(rank_rows, first_weight, preferred_element_type=jnp.float32)
    hidden = jax.nn.silu(pre_act).astype(jnp.bfloat16)
    logit_vec = jnp.dot(hidden, second_weight, preferred_element_type=jnp.float32)
    dlogit = live_mask * (jax.nn.sigmoid(logit_vec) - target)
    grad_two = jnp.dot(dlogit, hidden.astype(jnp.float32), precision=lax.Precision.HIGHEST)
    grad_pre = (
        dlogit[:, None] * second_weight.astype(jnp.float32)[None, :] * silu_grad(pre_act)
    ).astype(jnp.bfloat16)
    grad_one = jnp.dot(rank_rows.T, grad_pre, preferred_element_type=jnp.float32)
    return (live_mask * logit_vec, grad_one, grad_two)


def body(
    history,
    z_weight,
    xbc_weight,
    dt_weight,
    dt_bias,
    a_log,
    conv_weight,
    conv_bias,
    d_skip,
    norm_gain,
    out_weight,
    label_pos,
    label_count,
    label_value,
    item_feat,
    first_weight,
    second_weight,
):
    user_count, length, model_width = history.shape
    inner_width = z_weight.shape[1]
    head_count = a_log.shape[0]
    head_size = inner_width // head_count
    state_dim = (xbc_weight.shape[1] - inner_width) // 2
    tap_count = conv_weight.shape[0]
    flat_rows = history.reshape(user_count * length, model_width)
    z_gate = (
        jnp.dot(flat_rows, z_weight, preferred_element_type=jnp.float32)
        .astype(jnp.bfloat16)
        .reshape(user_count, length, inner_width)
    )
    xbc_raw = (
        jnp.dot(flat_rows, xbc_weight, preferred_element_type=jnp.float32)
        .astype(jnp.bfloat16)
        .reshape(user_count, length, -1)
    )
    step_size = jax.nn.softplus(
        jnp.dot(flat_rows, dt_weight, preferred_element_type=jnp.float32) + dt_bias
    ).reshape(user_count, length, head_count)
    rim_rows = passed_along(xbc_raw[:, length - (tap_count - 1) :, :], "tm", 1)
    padded = jnp.concatenate([rim_rows, xbc_raw], axis=1)
    conv_sum = jnp.zeros(xbc_raw.shape, jnp.float32) + conv_bias
    for tap in range(tap_count):
        conv_sum = conv_sum + conv_weight[tap] * padded[:, tap : tap + length, :].astype(
            jnp.float32
        )
    xbc = jax.nn.silu(conv_sum).astype(jnp.bfloat16)
    block_count = length // BLOCK
    x_part = xbc[..., :inner_width].reshape(user_count, block_count, BLOCK, head_count, head_size)
    b_part = xbc[..., inner_width : inner_width + state_dim].reshape(
        user_count, block_count, BLOCK, state_dim
    )
    c_part = xbc[..., inner_width + state_dim :].reshape(user_count, block_count, BLOCK, state_dim)
    log_decay = (-jnp.exp(a_log) * step_size).reshape(user_count, block_count, BLOCK, head_count)
    cumulated = jnp.cumsum(log_decay, axis=2)
    step_blocks = step_size.reshape(user_count, block_count, BLOCK, head_count)
    rows_idx = lax.broadcasted_iota(jnp.int32, (BLOCK, BLOCK), 0)
    cols_idx = lax.broadcasted_iota(jnp.int32, (BLOCK, BLOCK), 1)
    causal = (cols_idx <= rows_idx)[None, None]

    def block_step(carry_state, inputs):
        x_block, b_block, c_block, cum_block, step_block = inputs
        scores = jnp.einsum("utn,usn->uts", c_block, b_block, preferred_element_type=jnp.float32)
        cum_heads = jnp.swapaxes(cum_block, 1, 2)
        gaps = cum_heads[:, :, :, None] - cum_heads[:, :, None, :]
        decays = jnp.where(causal, jnp.exp(jnp.where(causal, gaps, 0.0)), 0.0)
        weights = (decays * jnp.swapaxes(step_block, 1, 2)[:, :, None, :] * scores[:, None]).astype(
            jnp.bfloat16
        )
        within = jnp.einsum("uhts,ushp->uthp", weights, x_block, preferred_element_type=jnp.float32)
        last_cum = cum_block[:, -1, :]
        carried = (
            (jnp.exp(last_cum[:, None, :] - cum_block) * step_block)[..., None]
            * x_block.astype(jnp.float32)
        ).astype(jnp.bfloat16)
        new_state = jnp.exp(last_cum)[:, :, None, None] * carry_state + jnp.einsum(
            "ushp,usn->uhpn", carried, b_block, preferred_element_type=jnp.float32
        )
        result = within + d_skip[None, None, :, None] * x_block.astype(jnp.float32)
        return (new_state, (result, carry_state))

    zero_state = jnp.zeros((user_count, head_count, head_size, state_dim), jnp.float32)
    scan_inputs = (
        jnp.moveaxis(x_part, 1, 0),
        jnp.moveaxis(b_part, 1, 0),
        jnp.moveaxis(c_part, 1, 0),
        jnp.moveaxis(cumulated, 1, 0),
        jnp.moveaxis(step_blocks, 1, 0),
    )
    local_end, (partial_value, entering_local) = lax.scan(block_step, zero_state, scan_inputs)
    block_last = cumulated[:, :, -1, :]
    before_log = jnp.cumsum(block_last, axis=1) - block_last
    chain_gain = jnp.exp(jnp.sum(block_last, axis=1))
    incoming = jnp.zeros_like(local_end)
    for relay_step in range(lax.axis_size("tm") - 1):
        outgoing = chain_gain[:, :, None, None] * incoming + local_end
        incoming = passed_along(outgoing, "tm", 1)
    entering = (
        jnp.moveaxis(entering_local, 0, 1)
        + jnp.exp(before_log)[..., None, None] * incoming[:, None]
    )
    entering_high = entering.astype(jnp.bfloat16)
    entering_low = (entering - entering_high.astype(jnp.float32)).astype(jnp.bfloat16)
    state_read = jnp.einsum(
        "ubtn,ubhpn->ubthp", c_part, entering_high, preferred_element_type=jnp.float32
    )
    state_read = state_read + jnp.einsum(
        "ubtn,ubhpn->ubthp", c_part, entering_low, preferred_element_type=jnp.float32
    )
    across = jnp.exp(cumulated)[..., None] * state_read
    ssd_out = (jnp.moveaxis(partial_value, 0, 1) + across).reshape(user_count, length, inner_width)
    gated_out = ssd_out * jax.nn.silu(z_gate.astype(jnp.float32))
    normed = (
        gated_out
        * lax.rsqrt(jnp.mean(gated_out * gated_out, axis=-1, keepdims=True) + 1e-05)
        * norm_gain
    ).astype(jnp.bfloat16)
    encoded = (
        jnp.dot(normed.reshape(-1, inner_width), out_weight, preferred_element_type=jnp.float32)
        .astype(jnp.bfloat16)
        .reshape(user_count, length, model_width)
    )
    slot_count = label_pos.shape[1]
    tm_index = lax.axis_index("tm")
    local_pos = label_pos - tm_index * length
    enc_rows = jax.vmap(lambda table, indices: table[indices])(encoded, local_pos)
    rank_rows = jnp.concatenate([enc_rows, item_feat], axis=-1)
    slot_iota = lax.broadcasted_iota(jnp.int32, (user_count, slot_count), 1)
    live_mask = (slot_iota < label_count).astype(jnp.float32)
    target = label_value.astype(jnp.float32)
    logit_vec, grad_one, grad_two = ranker(
        rank_rows.reshape(-1, 2 * model_width),
        target.reshape(-1),
        live_mask.reshape(-1),
        first_weight,
        second_weight,
    )
    row_logit = logit_vec.reshape(user_count, slot_count)
    share_first, share_second = (
        lax.psum_scatter(
            grad_one.astype(jnp.bfloat16), "tm", scatter_dimension=0, tiled=True
        ).astype(jnp.float32),
        lax.psum_scatter(
            grad_two.astype(jnp.bfloat16), "tm", scatter_dimension=0, tiled=True
        ).astype(jnp.float32),
    )
    summed_first, summed_second = (
        lax.psum(share_first.astype(jnp.bfloat16), "user").astype(jnp.float32),
        lax.psum(share_second.astype(jnp.bfloat16), "user").astype(jnp.float32),
    )
    grad_first, grad_second = (
        lax.all_gather(summed_first.astype(jnp.bfloat16), "tm", axis=0, tiled=True).astype(
            summed_first.dtype
        ),
        lax.all_gather(summed_second.astype(jnp.bfloat16), "tm", axis=0, tiled=True).astype(
            summed_second.dtype
        ),
    )
    return (encoded, row_logit, grad_first, grad_second)


def solution(mesh):
    in_specs = (
        P(("grp", "user"), "tm", None),
        P(),
        P(),
        P(),
        P(),
        P(),
        P(),
        P(),
        P(),
        P(),
        P(),
        P(("grp", "user"), "tm"),
        P(("grp", "user"), "tm"),
        P(("grp", "user"), "tm"),
        P(("grp", "user"), "tm", None),
        P(),
        P(),
    )
    out_specs = (P(("grp", "user"), "tm", None), P(("grp", "user"), "tm"), P("grp", None), P("grp"))
    return jax.shard_map(body, mesh=mesh, in_specs=in_specs, out_specs=out_specs, check_vma=False)
```

profile of v0, /device:TPU:0, one launch (start us, length us, event | category | flops | bytes accessed | tf_op | source)
XLA Modules:
  0.0 186.1 jit_solution(1924651855535223238)
XLA Ops:
  7.3 2.0 %convolution_convert_fusion = bf16[256,1280]{1,0:T(8,128)(2,1)S(1)} fusion(bf16[512,1280]{1,0:T(8,128)(2,1)} %param.19, bf16[1,256,512]{2,1,0:T(8,128)(2,1)} %param.17), kind=kOutput, calls=%fused_computation.2 | convolution fusion | flops 335872000 | bytes 2228224 | tf_op jit(solution)/shard_map/dot_general | solution.py:65
  9.4 2.4 %collective-permute-start = (bf16[1,3,1280]{2,1,0:T(4,128)(2,1)S(1)}, bf16[1,3,1280]{2,1,0:T(4,128)(2,1)S(1)}, u32[]{:S(2)}, u32[]{:S(2)}) collective-permute-start(bf16[1,3,1280]{2,1,0:T(4,128)(2,1)S(1)} %slice.63), channel_id=1, source_target_pairs={{0,1},{1,2},{2,3},{4,5},{5,6},{6,7},{8,9},{9,10},{10,11},{12,13},{... | collective-permute-start | bytes 23048 | tf_op jit(solution)/shard_map/ppermute | solution.py:12
  14.7 2.5 %copy.42 = f32[1,256,1024]{2,1,0:T(8,128)} copy(f32[1,256,1024]{1,2,0:T(8,128)} %bitcast.132) | data formatting | bytes 2097152 | tf_op jit(solution)/shard_map/while/body/eval_jaxpr/mul | solution.py:105
  19.6 1.4 convolution_add_fusion.1
  21.9 5.3 %collective-permute-start.1 = (f32[1,16,64,128]{3,2,1,0:T(8,128)}, f32[1,16,64,128]{3,2,1,0:T(8,128)}, u32[]{:S(2)}, u32[]{:S(2)}) collective-permute-start(f32[1,16,64,128]{3,2,1,0:T(8,128)} %add_bitcast_fusion), channel_id=1, source_target_pairs={{0,1},{1,2},{2,3},{4,5},{5,6},{6,7},{8,9},{9,10},{10,11},{12,13},{... | collective-permute-start | bytes 1572872 | tf_op jit(solution)/shard_map/ppermute | solution.py:12
  28.3 2.0 %bitcast_add_fusion.2 = f32[1,16,64,128]{3,2,1,0:T(8,128)} fusion(f32[16,64,128]{2,1,0:T(8,128)S(1)} %convolution_add_fusion.1, f32[1,16,64,128]{3,2,1,0:T(8,128)} %collective-permute-done.1, f32[16]{0:T(128)S(1)} %get-tuple-element.31), kind=kLoop, calls=%fused_computation.47 | loop fusion | flops 262144 | bytes 1572928 | tf_op jit(solution)/shard_map/add | solution.py:128
  30.3 7.3 %collective-permute-start.2 = (f32[1,16,64,128]{3,2,1,0:T(8,128)}, f32[1,16,64,128]{3,2,1,0:T(8,128)}, u32[]{:S(2)}, u32[]{:S(2)}) collective-permute-start(f32[1,16,64,128]{3,2,1,0:T(8,128)} %bitcast_add_fusion.2), channel_id=1, source_target_pairs={{0,1},{1,2},{2,3},{4,5},{5,6},{6,7},{8,9},{9,10},{10,11},{12,13},{... | collective-permute-start | bytes 1572872 | tf_op jit(solution)/shard_map/ppermute | solution.py:12
  38.3 1.3 slice_convert_fusion
  39.6 2.6 %copy.41 = f32[1,256,1024]{1,2,0:T(8,128)} copy(f32[1,256,1024]{2,1,0:T(8,128)} %get-tuple-element.45) | data formatting | bytes 2097152 | tf_op jit(solution)/shard_map/while/body/eval_jaxpr/convert_element_type | solution.py:106
  42.1 2.0 %copy.37 = bf16[1,256,1024]{1,2,0:T(8,128)(2,1)} copy(bf16[1,256,1024]{2,1,0:T(8,128)(2,1)} %get-tuple-element.46) | data formatting | bytes 1048576 | tf_op jit(solution)/shard_map/slice | solution.py:81
  45.4 3.6 %collective-permute-start.3 = (f32[1,16,64,128]{3,2,1,0:T(8,128)S(1)}, f32[1,16,64,128]{3,2,1,0:T(8,128)S(1)}, u32[]{:S(2)}, u32[]{:S(2)}) collective-permute-start(f32[1,16,64,128]{3,2,1,0:T(8,128)S(1)} %bitcast_add_fusion.1), channel_id=1, source_target_pairs={{0,1},{1,2},{2,3},{4,5},{5,6},{6,7},{8,9},{9,10},{10,11},{12,13},{... | collective-permute-start | bytes 1572872 | tf_op jit(solution)/shard_map/ppermute | solution.py:12
  49.2 2.8 %fusion.11 = f32[256,16,64]{0,2,1:T(8,128)S(1)} fusion(bf16[256,16,64]{0,2,1:T(8,128)(2,1)} %bitcast.138, f32[256,256]{1,0:T(8,128)S(1)} %fusion.38, f32[16,256]{1,0:T(8,128)S(1)} %bitcast.139, f32[16,256]{1,0:T(8,128)S(1)} %bitcast.142, pred[256,256]{1,0:T(8,128)(4,1)S(1)} %iota_compare_fusion, f32[1,256,16,64]{1,3,2,0:T(8,128)} %bitcast.135, ...), kind=kOutput, calls=%fused_computation.19 | convolution fusion | flops 141033472 | bytes 2981952 | tf_op jit(solution)/shard_map/while/body/eval_jaxpr/uhts,ushp->uthp/dot_general | solution.py:102
  52.4 1.4 fusion.9
  53.8 2.5 %copy.44 = f32[256,1024]{1,0:T(8,128)} copy(f32[256,1024]{0,1:T(8,128)} %bitcast.133) | data formatting | bytes 2097152 | tf_op jit(solution)/shard_map/reshape | solution.py:143
  56.4 2.3 %multiply_reduce_fusion = (f32[256]{0:T(256)S(1)}, f32[256,1024]{1,0:T(8,128)S(1)}) fusion(f32[256,1024]{1,0:T(8,128)} %copy.44, bf16[512,1024]{1,0:T(8,128)(2,1)} %param.18, bf16[1,256,512]{2,1,0:T(8,128)(2,1)S(1)} %copy-done.4), kind=kOutput, calls=%fused_computation.38 | convolution fusion | flops 270794496 | bytes 3408896 | tf_op jit(solution)/shard_map/dot_general | solution.py:60
  59.2 5.8 %gather_fusion = bf16[512,512]{1,0:T(8,128)(2,1)} fusion(bf16[1,256,512]{2,1,0:T(8,128)(2,1)S(1)} %fusion.12, s32[512]{0:T(512)S(1)} %bitcast.129), kind=kCustom, calls=%fused_computation | custom fusion | bytes 1052672 | tf_op jit(solution)/shard_map/vmap()/gather | solution.py:158
  65.0 2.8 %multiply_convert_fusion.3 = (bf16[512,1024]{1,0:T(8,128)(2,1)S(1)}, f32[512,1024]{1,0:T(8,128)S(1)}) fusion(bf16[1024,1024]{1,0:T(8,128)(2,1)S(1)} %copy-done, bf16[1,512,512]{2,1,0:T(8,128)(2,1)} %param.31, bf16[1,512,512]{2,1,0:T(8,128)(2,1)} %bitcast.136), kind=kOutput, calls=%fused_computation.5 | convolution fusion | flops 1078460416 | bytes 6291456 | tf_op jit(solution)/shard_map/dot_general | solution.py:21
  68.8 3.0 %convolution_convert_fusion.1 = bf16[1024,1024]{1,0:T(8,128)(2,1)} fusion(f32[512,1024]{1,0:T(8,128)S(1)} %get-tuple-element.52, f32[1024]{0:T(1024)S(1)} %convert_element_type.159, f32[512]{0:T(512)S(1)} %get-tuple-element.47, bf16[1,512,512]{2,1,0:T(8,128)(2,1)S(1)} %copy-done.15, bf16[1,512,512]{2,1,0:T(8,128)(2,1)S(1)} %bitcast.137), kind=kOutput, calls=%fused_computation.13 | convolution fusion | flops 1082130432 | bytes 5249024 | tf_op jit(solution)/shard_map/dot_general | solution.py:29
  71.9 38.7 %reduce-scatter.2.cloned.1.call-done = bf16[256,1024]{1,0:T(8,128)(2,1)} async-done(((bf16[1024,1024]{1,0:T(8,128)(2,1)}), bf16[256,1024]{1,0:T(8,128)(2,1)}) %reduce-scatter.2.cloned.1.call-update) | async-done | bytes 524304 | tf_op jit(solution)/shard_map/reduce_scatter | solution.py:172
  110.7 40.8 %all-reduce.3.cloned.1.call-done = bf16[256,1024]{1,0:T(8,128)(2,1)} async-done(((bf16[256,1024]{1,0:T(8,128)(2,1)}), bf16[256,1024]{1,0:T(8,128)(2,1)}) %all-reduce.3.cloned.1.call-update) | async-done | bytes 524304 | tf_op jit(solution)/shard_map/psum | solution.py:180
  153.3 5.6 %all-reduce = bf16[1024]{0:T(1024)(128)(2,1)S(1)} all-reduce(bf16[1024]{0:T(1024)(128)(2,1)S(1)} %convert_element_type.163), channel_id=3, replica_groups=mesh['grp'=2,'user'=4,'tm'=4] {'tm'}, use_global_device_ids=true, to_apply=%region_5.6.clone | all-reduce | flops 1024 | bytes 4096
  159.0 10.6 %psum.15 = bf16[256]{0:T(256)(128)(2,1)S(1)} all-reduce(bf16[256]{0:T(256)(128)(2,1)S(1)} %dynamic-slice.4), channel_id=1, replica_groups=mesh['grp'=2,'user'=4,'tm'=4] {'user'}, use_global_device_ids=true, to_apply=%region_6.7 | all-reduce | flops 256 | bytes 1024 | tf_op jit(solution)/shard_map/psum | solution.py:181
  169.6 5.1 %all-gather = bf16[4,1,256]{2,1,0:T(2,128)(2,1)S(1)} all-gather(bf16[1,1,256]{2,1,0:T(2,128)(2,1)S(1)} %reshape.326), channel_id=1, replica_groups=mesh['grp'=2,'user'=4,'tm'=4] {'tm'}, dimensions={0}, use_global_device_ids=true | all-gather | bytes 2560 | tf_op jit(solution)/shard_map/all_gather | solution.py:187
  175.5 4.1 %convert_element_type.162 = f32[1024,1024]{1,0:T(8,128)} convert(bf16[1024,1024]{1,0:T(8,128)(2,1)} %all-gather.3.cloned.1.call-done) | non-fusion elementwise | flops 1048576 | bytes 6291456 | tf_op jit(solution)/shard_map/convert_element_type | solution.py:184
  (92 shorter events, 12.5 us)
Async XLA Ops:
  7.2 57.8 %copy-start = (bf16[1024,1024]{1,0:T(8,128)(2,1)S(1)}, bf16[1024,1024]{1,0:T(8,128)(2,1)}, u32[]{:S(2)}) copy-start(bf16[1024,1024]{1,0:T(8,128)(2,1)} %param.32) | copy-start | bytes 6291460
  7.2 4.6 %copy-start.3 = (bf16[1,256,512]{2,1,0:T(8,128)(2,1)S(1)}, bf16[1,256,512]{2,1,0:T(8,128)(2,1)}, u32[]{:S(2)}) copy-start(bf16[1,256,512]{2,1,0:T(8,128)(2,1)} %param.17) | copy-start | bytes 786436
  7.2 4.6 %copy-start.16 = (f32[16]{0:T(128)S(1)}, f32[16]{0:T(128)}, u32[]{:S(2)}) copy-start(f32[16]{0:T(128)} %param.22) | copy-start | bytes 196
  7.2 4.6 %copy-start.14 = (f32[16]{0:T(128)S(1)}, f32[16]{0:T(128)}, u32[]{:S(2)}) copy-start(f32[16]{0:T(128)} %param.21) | copy-start | bytes 196
  7.2 4.6 %copy-start.8 = (bf16[512,16]{0,1:T(8,128)(2,1)S(1)}, bf16[512,16]{0,1:T(8,128)(2,1)}, u32[]{:S(2)}) copy-start(bf16[512,16]{0,1:T(8,128)(2,1)} %param.20) | copy-start | bytes 49156
  7.2 6.4 %copy-start.7 = (f32[4,1280]{1,0:T(4,128)S(1)}, f32[4,1280]{1,0:T(4,128)}, u32[]{:S(2)}) copy-start(f32[4,1280]{1,0:T(4,128)} %param.23) | copy-start | bytes 61444
  7.2 103.4 %reduce-scatter.2.cloned.1.call-start = ((), (), s32[]{:S(2)}) async-start(), calls=%async_computation.1 | async-start | bytes 2621440 | tf_op jit(solution)/shard_map/reduce_scatter | solution.py:172
  9.3 7.9 %copy-start.9 = (f32[1280]{0:T(1024)S(1)}, f32[1280]{0:T(1024)}, u32[]{:S(2)}) copy-start(f32[1280]{0:T(1024)} %param.24) | copy-start | bytes 15364
  9.4 7.9 %collective-permute-start = (bf16[1,3,1280]{2,1,0:T(4,128)(2,1)S(1)}, bf16[1,3,1280]{2,1,0:T(4,128)(2,1)S(1)}, u32[]{:S(2)}, u32[]{:S(2)}) collective-permute-start(bf16[1,3,1280]{2,1,0:T(4,128)(2,1)S(1)} %slice.63), channel_id=1, source_target_pairs={{0,1},{1,2},{2,3},{4,5},{5,6},{6,7},{8,9},{9,10},{10,11},{12,13},{... | collective-permute-start | bytes 23048 | tf_op jit(solution)/shard_map/ppermute | solution.py:12
  18.6 8.6 %copy-start.12 = (s32[1,512]{1,0:T(1,128)S(1)}, s32[1,512]{1,0:T(1,128)}, u32[]{:S(2)}) copy-start(s32[1,512]{1,0:T(1,128)} %param.28) | copy-start | bytes 6148
  19.6 17.9 %copy-start.10 = (bf16[1024]{0:T(1024)(128)(2,1)S(1)}, bf16[1024]{0:T(1024)(128)(2,1)}, u32[]{:S(2)}) copy-start(bf16[1024]{0:T(1024)(128)(2,1)} %param.33) | copy-start | bytes 6148
  19.6 18.6 %copy-start.13 = (s32[1,512]{1,0:T(1,128)S(1)}, s32[1,512]{1,0:T(1,128)}, u32[]{:S(2)}) copy-start(s32[1,512]{1,0:T(1,128)} %param.30) | copy-start | bytes 6148
  21.9 6.3 %collective-permute-start.1 = (f32[1,16,64,128]{3,2,1,0:T(8,128)}, f32[1,16,64,128]{3,2,1,0:T(8,128)}, u32[]{:S(2)}, u32[]{:S(2)}) collective-permute-start(f32[1,16,64,128]{3,2,1,0:T(8,128)} %add_bitcast_fusion), channel_id=1, source_target_pairs={{0,1},{1,2},{2,3},{4,5},{5,6},{6,7},{8,9},{9,10},{10,11},{12,13},{... | collective-permute-start | bytes 1572872 | tf_op jit(solution)/shard_map/ppermute | solution.py:12
  30.3 13.9 %collective-permute-start.2 = (f32[1,16,64,128]{3,2,1,0:T(8,128)}, f32[1,16,64,128]{3,2,1,0:T(8,128)}, u32[]{:S(2)}, u32[]{:S(2)}) collective-permute-start(f32[1,16,64,128]{3,2,1,0:T(8,128)} %bitcast_add_fusion.2), channel_id=1, source_target_pairs={{0,1},{1,2},{2,3},{4,5},{5,6},{6,7},{8,9},{9,10},{10,11},{12,13},{... | collective-permute-start | bytes 1572872 | tf_op jit(solution)/shard_map/ppermute | solution.py:12
  39.6 9.6 %copy-start.17 = (f32[16]{0:T(128)S(1)}, f32[16]{0:T(128)}, u32[]{:S(2)}) copy-start(f32[16]{0:T(128)} %param.25) | copy-start | bytes 196
  45.4 6.7 %collective-permute-start.3 = (f32[1,16,64,128]{3,2,1,0:T(8,128)S(1)}, f32[1,16,64,128]{3,2,1,0:T(8,128)S(1)}, u32[]{:S(2)}, u32[]{:S(2)}) collective-permute-start(f32[1,16,64,128]{3,2,1,0:T(8,128)S(1)} %bitcast_add_fusion.1), channel_id=1, source_target_pairs={{0,1},{1,2},{2,3},{4,5},{5,6},{6,7},{8,9},{9,10},{10,11},{12,13},{... | collective-permute-start | bytes 1572872 | tf_op jit(solution)/shard_map/ppermute | solution.py:12
  52.4 4.0 %copy-start.4 = (bf16[1,256,512]{2,1,0:T(8,128)(2,1)S(1)}, bf16[1,256,512]{2,1,0:T(8,128)(2,1)}, u32[]{:S(2)}) copy-start(bf16[1,256,512]{2,1,0:T(8,128)(2,1)} %param.17) | copy-start | bytes 786436
  56.4 2.3 %copy-start.11 = (f32[1024]{0:T(1024)S(1)}, f32[1024]{0:T(1024)}, u32[]{:S(2)}) copy-start(f32[1024]{0:T(1024)} %param.26) | copy-start | bytes 12292
  59.2 5.8 %copy-start.1 = (bf16[1,256,512]{2,1,0:T(8,128)(2,1)}, bf16[1,256,512]{2,1,0:T(8,128)(2,1)S(1)}, u32[]{:S(2)}) copy-start(bf16[1,256,512]{2,1,0:T(8,128)(2,1)S(1)} %fusion.12) | copy-start | bytes 786436
  65.0 3.8 %copy-start.6 = (bf16[512,512]{1,0:T(8,128)(2,1)S(1)}, bf16[512,512]{1,0:T(8,128)(2,1)}, u32[]{:S(2)}) copy-start(bf16[512,512]{1,0:T(8,128)(2,1)} %gather_fusion) | copy-start | bytes 1572868
  65.0 3.8 %copy-start.15 = (bf16[1,512,512]{2,1,0:T(8,128)(2,1)S(1)}, bf16[1,512,512]{2,1,0:T(8,128)(2,1)}, u32[]{:S(2)}) copy-start(bf16[1,512,512]{2,1,0:T(8,128)(2,1)} %param.31) | copy-start | bytes 1572868
  71.8 79.7 %copy-start.18 = (u32[32]{0:T(128)S(1)}, u32[32]{0:T(128)}, u32[]{:S(2)}) copy-start(u32[32]{0:T(128)} %constant.78) | copy-start | bytes 388
  71.8 79.6 %all-reduce.3.cloned.1.call-start = ((), (), s32[]{:S(2)}) async-start(), calls=%async_computation.2 | async-start | bytes 1048576 | tf_op jit(solution)/shard_map/psum | solution.py:180
  110.6 64.9 %all-gather.3.cloned.1.call-start = ((), (), s32[]{:S(2)}) async-start(), calls=%async_computation.3 | async-start | bytes 2621440 | tf_op jit(solution)/shard_map/all_gather | solution.py:184
  (2 other events, 3.5 us)
Sparse Core Ops, SparseCore 0:
  72.0 38.5 reduce-scatter.1
  112.9 38.4 all-reduce.2
  153.0 22.3 all-gather.2
where the time goes:
time: 187 us; the launch traced here: 186 us
  waiting for transfers between devices  80.8 us (43%)
  blocking collectives  21.3 us (11%)
  local copies, waits for them, and re-layouts  19.2 us (10%)
  starting transfers between devices  18.7 us (10%)
  matrix products  17.8 us (10%)
  between operations  15.4 us (8%)
  other arithmetic  12.8 us (7%)
    psum x1, waiting for transfers between devices, body(): lax.psum(share_first.astype(jnp.bfloat16), 'user').astype(jnp.float32)  40.8 us
    reduce_scatter x1, waiting for transfers between devices, body(): lax.psum_scatter(grad_one.astype(jnp.bfloat16), 'tm', scatter_dimension=0...  38.7 us
    ppermute x4, starting transfers between devices, passed_along(): return lax.ppermute(shard, axis, pairs)  18.6 us
    psum x1, blocking collectives, body(): lax.psum(share_second.astype(jnp.bfloat16), 'user').astype(jnp.float32)  10.6 us
    gather x2, local copies, waits for them, and re-layouts, body(): table[indices]  5.84 us
    unnamed x1, blocking collectives  5.65 us
    all_gather x1, blocking collectives, body(): lax.all_gather(summed_second.astype(jnp.bfloat16), 'tm', axis=0, tiled=True)  5.13 us
    convert_element_type x1, other arithmetic, body(): lax.all_gather(summed_first.astype(jnp.bfloat16), 'tm', axis=0, tiled=True)  4.07 us
  transfers between devices with their start and end apart: 7, of which 4 were waited for; matrix products, arithmetic and copies ran while one was open for 9% of the time, Pallas kernels for 0%

commit v1 on v0

--- a/solution.py
+++ b/solution.py
@@ -177,7 +177,9 @@
         ).astype(jnp.float32),
     )
     summed_first, summed_second = (
-        lax.psum(share_first.astype(jnp.bfloat16), "user").astype(jnp.float32),
+        jnp.sum(lax.all_gather(share_first.astype(jnp.bfloat16), "user"), axis=0).astype(
+            jnp.float32
+        ),
         lax.psum(share_second.astype(jnp.bfloat16), "user").astype(jnp.float32),
     )
     grad_first, grad_second = (

time: 187 us -> 196 us (1.048)
  waiting for transfers between devices: 80.8 us -> 87 us
  other arithmetic: 12.8 us -> 15.7 us
    all_gather x0 -> x1, waiting for transfers between devices: none -> 47.2 us  [body(): lax.all_gather(share_first.astype(jnp.bfloat16), 'user')]
    psum x1 -> x0, waiting for transfers between devices: 40.8 us -> none  [body(): lax.psum(share_first.astype(jnp.bfloat16), 'user').astype(jnp.float32)]
    reduce_sum x0 -> x1, other arithmetic: none -> 2.92 us  [body(): jnp.sum(lax.all_gather(share_first.astype(jnp.bfloat16), 'user'), axis=0)]
  transfers between devices with their start and end apart: 7 -> 7, of which waited for: 4 -> 3; matrix products, arithmetic and copies ran while one was open for 9% -> 8% of each run, Pallas kernels for 0% -> 0%
where the time goes in v1:
time: 196 us; the launch traced here: 195 us
  waiting for transfers between devices  87 us (44%)
  blocking collectives  21.4 us (11%)
  local copies, waits for them, and re-layouts  19.2 us (10%)
  starting transfers between devices  18.7 us (10%)
  matrix products  17.8 us (9%)
  other arithmetic  15.7 us (8%)
  between operations  15.5 us (8%)
    all_gather x1, waiting for transfers between devices, body(): lax.all_gather(share_first.astype(jnp.bfloat16), 'user')  47.2 us
    reduce_scatter x1, waiting for transfers between devices, body(): lax.psum_scatter(grad_one.astype(jnp.bfloat16), 'tm', scatter_dimension=0...  38.7 us
    ppermute x4, starting transfers between devices, passed_along(): return lax.ppermute(shard, axis, pairs)  18.6 us
    psum x1, blocking collectives, body(): lax.psum(share_second.astype(jnp.bfloat16), 'user').astype(jnp.float32)  9.94 us
    unnamed x1, blocking collectives  6.37 us
    gather x2, local copies, waits for them, and re-layouts, body(): table[indices]  5.84 us
    all_gather x1, blocking collectives, body(): lax.all_gather(summed_second.astype(jnp.bfloat16), 'tm', axis=0, tiled=True)  5.06 us
    convert_element_type x1, other arithmetic, body(): lax.all_gather(summed_first.astype(jnp.bfloat16), 'tm', axis=0, tiled=True)  4.07 us
  transfers between devices with their start and end apart: 7, of which 3 were waited for; matrix products, arithmetic and copies ran while one was open for 8% of the time, Pallas kernels for 0%

profile of v1, /device:TPU:0, one launch (start us, length us, event | category | flops | bytes accessed | tf_op | source)
XLA Modules:
  0.0 195.2 jit_solution(10576400393051169997)
XLA Ops:
  7.3 2.0 %convolution_convert_fusion = bf16[256,1280]{1,0:T(8,128)(2,1)S(1)} fusion(bf16[512,1280]{1,0:T(8,128)(2,1)} %param.19, bf16[1,256,512]{2,1,0:T(8,128)(2,1)} %param.17), kind=kOutput, calls=%fused_computation.2 | convolution fusion | flops 335872000 | bytes 2228224 | tf_op jit(solution)/shard_map/dot_general | solution.py:65
  9.4 2.4 %collective-permute-start = (bf16[1,3,1280]{2,1,0:T(4,128)(2,1)S(1)}, bf16[1,3,1280]{2,1,0:T(4,128)(2,1)S(1)}, u32[]{:S(2)}, u32[]{:S(2)}) collective-permute-start(bf16[1,3,1280]{2,1,0:T(4,128)(2,1)S(1)} %slice.63), channel_id=1, source_target_pairs={{0,1},{1,2},{2,3},{4,5},{5,6},{6,7},{8,9},{9,10},{10,11},{12,13},{... | collective-permute-start | bytes 23048 | tf_op jit(solution)/shard_map/ppermute | solution.py:12
  14.7 2.5 %copy.42 = f32[1,256,1024]{2,1,0:T(8,128)} copy(f32[1,256,1024]{1,2,0:T(8,128)} %bitcast.133) | data formatting | bytes 2097152 | tf_op jit(solution)/shard_map/while/body/eval_jaxpr/mul | solution.py:105
  19.6 1.4 convolution_add_fusion.1
  21.9 5.3 %collective-permute-start.1 = (f32[1,16,64,128]{3,2,1,0:T(8,128)}, f32[1,16,64,128]{3,2,1,0:T(8,128)}, u32[]{:S(2)}, u32[]{:S(2)}) collective-permute-start(f32[1,16,64,128]{3,2,1,0:T(8,128)} %add_bitcast_fusion), channel_id=1, source_target_pairs={{0,1},{1,2},{2,3},{4,5},{5,6},{6,7},{8,9},{9,10},{10,11},{12,13},{... | collective-permute-start | bytes 1572872 | tf_op jit(solution)/shard_map/ppermute | solution.py:12
  28.3 2.0 %bitcast_add_fusion.2 = f32[1,16,64,128]{3,2,1,0:T(8,128)} fusion(f32[16,64,128]{2,1,0:T(8,128)S(1)} %convolution_add_fusion.1, f32[1,16,64,128]{3,2,1,0:T(8,128)} %collective-permute-done.1, f32[16]{0:T(128)S(1)} %get-tuple-element.31), kind=kLoop, calls=%fused_computation.47 | loop fusion | flops 262144 | bytes 1572928 | tf_op jit(solution)/shard_map/add | solution.py:128
  30.3 7.3 %collective-permute-start.2 = (f32[1,16,64,128]{3,2,1,0:T(8,128)}, f32[1,16,64,128]{3,2,1,0:T(8,128)}, u32[]{:S(2)}, u32[]{:S(2)}) collective-permute-start(f32[1,16,64,128]{3,2,1,0:T(8,128)} %bitcast_add_fusion.2), channel_id=1, source_target_pairs={{0,1},{1,2},{2,3},{4,5},{5,6},{6,7},{8,9},{9,10},{10,11},{12,13},{... | collective-permute-start | bytes 1572872 | tf_op jit(solution)/shard_map/ppermute | solution.py:12
  39.6 2.6 %copy.41 = f32[1,256,1024]{1,2,0:T(8,128)} copy(f32[1,256,1024]{2,1,0:T(8,128)} %get-tuple-element.45) | data formatting | bytes 2097152 | tf_op jit(solution)/shard_map/while/body/eval_jaxpr/convert_element_type | solution.py:106
  42.1 2.0 %copy.37 = bf16[1,256,1024]{1,2,0:T(8,128)(2,1)} copy(bf16[1,256,1024]{2,1,0:T(8,128)(2,1)} %get-tuple-element.46) | data formatting | bytes 1048576 | tf_op jit(solution)/shard_map/slice | solution.py:81
  45.4 3.6 %collective-permute-start.3 = (f32[1,16,64,128]{3,2,1,0:T(8,128)S(1)}, f32[1,16,64,128]{3,2,1,0:T(8,128)S(1)}, u32[]{:S(2)}, u32[]{:S(2)}) collective-permute-start(f32[1,16,64,128]{3,2,1,0:T(8,128)S(1)} %bitcast_add_fusion.1), channel_id=1, source_target_pairs={{0,1},{1,2},{2,3},{4,5},{5,6},{6,7},{8,9},{9,10},{10,11},{12,13},{... | collective-permute-start | bytes 1572872 | tf_op jit(solution)/shard_map/ppermute | solution.py:12
  49.2 2.8 %fusion.11 = f32[256,16,64]{0,2,1:T(8,128)S(1)} fusion(bf16[256,16,64]{0,2,1:T(8,128)(2,1)} %bitcast.140, f32[256,256]{1,0:T(8,128)S(1)} %fusion.38, f32[16,256]{1,0:T(8,128)S(1)} %bitcast.141, f32[16,256]{1,0:T(8,128)S(1)} %bitcast.144, pred[256,256]{1,0:T(8,128)(4,1)S(1)} %iota_compare_fusion, f32[1,256,16,64]{1,3,2,0:T(8,128)} %bitcast.137, ...), kind=kOutput, calls=%fused_computation.19 | convolution fusion | flops 141033472 | bytes 2981952 | tf_op jit(solution)/shard_map/while/body/eval_jaxpr/uhts,ushp->uthp/dot_general | solution.py:102
  52.4 1.4 fusion.9
  53.8 2.5 %copy.44 = f32[256,1024]{1,0:T(8,128)} copy(f32[256,1024]{0,1:T(8,128)} %bitcast.134) | data formatting | bytes 2097152 | tf_op jit(solution)/shard_map/reshape | solution.py:143
  56.4 2.3 %multiply_reduce_fusion = (f32[256]{0:T(256)S(1)}, f32[256,1024]{1,0:T(8,128)S(1)}) fusion(f32[256,1024]{1,0:T(8,128)} %copy.44, bf16[512,1024]{1,0:T(8,128)(2,1)} %param.18, bf16[1,256,512]{2,1,0:T(8,128)(2,1)S(1)} %copy-done.4), kind=kOutput, calls=%fused_computation.38 | convolution fusion | flops 270794496 | bytes 3408896 | tf_op jit(solution)/shard_map/dot_general | solution.py:60
  59.2 5.8 %gather_fusion = bf16[512,512]{1,0:T(8,128)(2,1)} fusion(bf16[1,256,512]{2,1,0:T(8,128)(2,1)S(1)} %fusion.12, s32[512]{0:T(512)S(1)} %bitcast.130), kind=kCustom, calls=%fused_computation | custom fusion | bytes 1052672 | tf_op jit(solution)/shard_map/vmap()/gather | solution.py:158
  65.0 2.8 %multiply_convert_fusion.3 = (bf16[512,1024]{1,0:T(8,128)(2,1)S(1)}, f32[512,1024]{1,0:T(8,128)S(1)}) fusion(bf16[1024,1024]{1,0:T(8,128)(2,1)S(1)} %copy-done, bf16[1,512,512]{2,1,0:T(8,128)(2,1)} %param.31, bf16[1,512,512]{2,1,0:T(8,128)(2,1)} %bitcast.138), kind=kOutput, calls=%fused_computation.5 | convolution fusion | flops 1078460416 | bytes 6291456 | tf_op jit(solution)/shard_map/dot_general | solution.py:21
  68.8 3.0 %convolution_convert_fusion.1 = bf16[1024,1024]{1,0:T(8,128)(2,1)} fusion(f32[512,1024]{1,0:T(8,128)S(1)} %get-tuple-element.52, f32[1024]{0:T(1024)S(1)} %convert_element_type.161, f32[512]{0:T(512)S(1)} %get-tuple-element.47, bf16[1,512,512]{2,1,0:T(8,128)(2,1)S(1)} %copy-done.15, bf16[1,512,512]{2,1,0:T(8,128)(2,1)S(1)} %bitcast.139), kind=kOutput, calls=%fused_computation.13 | convolution fusion | flops 1082130432 | bytes 5249024 | tf_op jit(solution)/shard_map/dot_general | solution.py:29
  71.9 38.7 %reduce-scatter.2.cloned.1.call-done = bf16[256,1024]{1,0:T(8,128)(2,1)} async-done(((bf16[1024,1024]{1,0:T(8,128)(2,1)}), bf16[256,1024]{1,0:T(8,128)(2,1)}) %reduce-scatter.2.cloned.1.call-update) | async-done | bytes 524304 | tf_op jit(solution)/shard_map/reduce_scatter | solution.py:172
  110.7 47.2 %all-gather.7.cloned.1.call-done = bf16[1024,1024]{1,0:T(8,128)(2,1)} async-done(((bf16[256,1024]{1,0:T(8,128)(2,1)}), bf16[1024,1024]{1,0:T(8,128)(2,1)}) %all-gather.7.cloned.1.call-update) | async-done | bytes 2097168 | tf_op jit(solution)/shard_map/all_gather | solution.py:180
  157.8 2.9 %reduce_sum.26 = bf16[256,1024]{1,0:T(8,128)(2,1)} reduce(bf16[4,256,1024]{2,1,0:T(8,128)(2,1)} %bitcast.135, bf16[]{:T(256)} %constant.58.clone.1), dimensions={0}, to_apply=%region_4.5 | reduce | flops 786432 | bytes 2621442 | tf_op jit(solution)/shard_map/reduce_sum | solution.py:180
  162.6 6.4 %all-reduce = bf16[1024]{0:T(1024)(128)(2,1)S(1)} all-reduce(bf16[1024]{0:T(1024)(128)(2,1)S(1)} %convert_element_type.165), channel_id=4, replica_groups=mesh['grp'=2,'user'=4,'tm'=4] {'tm'}, use_global_device_ids=true, to_apply=%region_5.6.clone | all-reduce | flops 1024 | bytes 4096
  169.0 9.9 %psum.7 = bf16[256]{0:T(256)(128)(2,1)S(1)} all-reduce(bf16[256]{0:T(256)(128)(2,1)S(1)} %dynamic-slice.4), channel_id=1, replica_groups=mesh['grp'=2,'user'=4,'tm'=4] {'user'}, use_global_device_ids=true, to_apply=%region_6.7 | all-reduce | flops 256 | bytes 1024 | tf_op jit(solution)/shard_map/psum | solution.py:183
  179.0 5.1 %all-gather.1 = bf16[4,1,256]{2,1,0:T(2,128)(2,1)S(1)} all-gather(bf16[1,1,256]{2,1,0:T(2,128)(2,1)S(1)} %reshape.327), channel_id=1, replica_groups=mesh['grp'=2,'user'=4,'tm'=4] {'tm'}, dimensions={0}, use_global_device_ids=true | all-gather | bytes 2560 | tf_op jit(solution)/shard_map/all_gather | solution.py:189
  184.6 4.1 %convert_element_type.164 = f32[1024,1024]{1,0:T(8,128)} convert(bf16[1024,1024]{1,0:T(8,128)(2,1)} %all-gather.5.cloned.1.call-done) | non-fusion elementwise | flops 1048576 | bytes 6291456 | tf_op jit(solution)/shard_map/convert_element_type | solution.py:186
  (93 shorter events, 13.7 us)
Async XLA Ops:
  7.2 57.8 %copy-start = (bf16[1024,1024]{1,0:T(8,128)(2,1)S(1)}, bf16[1024,1024]{1,0:T(8,128)(2,1)}, u32[]{:S(2)}) copy-start(bf16[1024,1024]{1,0:T(8,128)(2,1)} %param.32) | copy-start | bytes 6291460
  7.2 4.6 %copy-start.3 = (bf16[1,256,512]{2,1,0:T(8,128)(2,1)S(1)}, bf16[1,256,512]{2,1,0:T(8,128)(2,1)}, u32[]{:S(2)}) copy-start(bf16[1,256,512]{2,1,0:T(8,128)(2,1)} %param.17) | copy-start | bytes 786436
  7.2 4.6 %copy-start.16 = (f32[16]{0:T(128)S(1)}, f32[16]{0:T(128)}, u32[]{:S(2)}) copy-start(f32[16]{0:T(128)} %param.22) | copy-start | bytes 196
  7.2 4.6 %copy-start.14 = (f32[16]{0:T(128)S(1)}, f32[16]{0:T(128)}, u32[]{:S(2)}) copy-start(f32[16]{0:T(128)} %param.21) | copy-start | bytes 196
  7.2 4.6 %copy-start.8 = (bf16[512,16]{0,1:T(8,128)(2,1)S(1)}, bf16[512,16]{0,1:T(8,128)(2,1)}, u32[]{:S(2)}) copy-start(bf16[512,16]{0,1:T(8,128)(2,1)} %param.20) | copy-start | bytes 49156
  7.2 6.4 %copy-start.7 = (f32[4,1280]{1,0:T(4,128)S(1)}, f32[4,1280]{1,0:T(4,128)}, u32[]{:S(2)}) copy-start(f32[4,1280]{1,0:T(4,128)} %param.23) | copy-start | bytes 61444
  7.2 103.3 %reduce-scatter.2.cloned.1.call-start = ((), (), s32[]{:S(2)}) async-start(), calls=%async_computation.1 | async-start | bytes 2621440 | tf_op jit(solution)/shard_map/reduce_scatter | solution.py:172
  9.3 7.9 %copy-start.9 = (f32[1280]{0:T(1024)S(1)}, f32[1280]{0:T(1024)}, u32[]{:S(2)}) copy-start(f32[1280]{0:T(1024)} %param.24) | copy-start | bytes 15364
  9.4 7.9 %collective-permute-start = (bf16[1,3,1280]{2,1,0:T(4,128)(2,1)S(1)}, bf16[1,3,1280]{2,1,0:T(4,128)(2,1)S(1)}, u32[]{:S(2)}, u32[]{:S(2)}) collective-permute-start(bf16[1,3,1280]{2,1,0:T(4,128)(2,1)S(1)} %slice.63), channel_id=1, source_target_pairs={{0,1},{1,2},{2,3},{4,5},{5,6},{6,7},{8,9},{9,10},{10,11},{12,13},{... | collective-permute-start | bytes 23048 | tf_op jit(solution)/shard_map/ppermute | solution.py:12
  18.6 8.6 %copy-start.12 = (s32[1,512]{1,0:T(1,128)S(1)}, s32[1,512]{1,0:T(1,128)}, u32[]{:S(2)}) copy-start(s32[1,512]{1,0:T(1,128)} %param.28) | copy-start | bytes 6148
  19.6 17.9 %copy-start.10 = (bf16[1024]{0:T(1024)(128)(2,1)S(1)}, bf16[1024]{0:T(1024)(128)(2,1)}, u32[]{:S(2)}) copy-start(bf16[1024]{0:T(1024)(128)(2,1)} %param.33) | copy-start | bytes 6148
  19.6 18.6 %copy-start.13 = (s32[1,512]{1,0:T(1,128)S(1)}, s32[1,512]{1,0:T(1,128)}, u32[]{:S(2)}) copy-start(s32[1,512]{1,0:T(1,128)} %param.30) | copy-start | bytes 6148
  21.9 6.3 %collective-permute-start.1 = (f32[1,16,64,128]{3,2,1,0:T(8,128)}, f32[1,16,64,128]{3,2,1,0:T(8,128)}, u32[]{:S(2)}, u32[]{:S(2)}) collective-permute-start(f32[1,16,64,128]{3,2,1,0:T(8,128)} %add_bitcast_fusion), channel_id=1, source_target_pairs={{0,1},{1,2},{2,3},{4,5},{5,6},{6,7},{8,9},{9,10},{10,11},{12,13},{... | collective-permute-start | bytes 1572872 | tf_op jit(solution)/shard_map/ppermute | solution.py:12
  30.3 13.9 %collective-permute-start.2 = (f32[1,16,64,128]{3,2,1,0:T(8,128)}, f32[1,16,64,128]{3,2,1,0:T(8,128)}, u32[]{:S(2)}, u32[]{:S(2)}) collective-permute-start(f32[1,16,64,128]{3,2,1,0:T(8,128)} %bitcast_add_fusion.2), channel_id=1, source_target_pairs={{0,1},{1,2},{2,3},{4,5},{5,6},{6,7},{8,9},{9,10},{10,11},{12,13},{... | collective-permute-start | bytes 1572872 | tf_op jit(solution)/shard_map/ppermute | solution.py:12
  39.6 9.6 %copy-start.17 = (f32[16]{0:T(128)S(1)}, f32[16]{0:T(128)}, u32[]{:S(2)}) copy-start(f32[16]{0:T(128)} %param.25) | copy-start | bytes 196
  45.4 6.7 %collective-permute-start.3 = (f32[1,16,64,128]{3,2,1,0:T(8,128)S(1)}, f32[1,16,64,128]{3,2,1,0:T(8,128)S(1)}, u32[]{:S(2)}, u32[]{:S(2)}) collective-permute-start(f32[1,16,64,128]{3,2,1,0:T(8,128)S(1)} %bitcast_add_fusion.1), channel_id=1, source_target_pairs={{0,1},{1,2},{2,3},{4,5},{5,6},{6,7},{8,9},{9,10},{10,11},{12,13},{... | collective-permute-start | bytes 1572872 | tf_op jit(solution)/shard_map/ppermute | solution.py:12
  52.4 4.0 %copy-start.4 = (bf16[1,256,512]{2,1,0:T(8,128)(2,1)S(1)}, bf16[1,256,512]{2,1,0:T(8,128)(2,1)}, u32[]{:S(2)}) copy-start(bf16[1,256,512]{2,1,0:T(8,128)(2,1)} %param.17) | copy-start | bytes 786436
  56.4 2.3 %copy-start.11 = (f32[1024]{0:T(1024)S(1)}, f32[1024]{0:T(1024)}, u32[]{:S(2)}) copy-start(f32[1024]{0:T(1024)} %param.26) | copy-start | bytes 12292
  59.2 5.8 %copy-start.1 = (bf16[1,256,512]{2,1,0:T(8,128)(2,1)}, bf16[1,256,512]{2,1,0:T(8,128)(2,1)S(1)}, u32[]{:S(2)}) copy-start(bf16[1,256,512]{2,1,0:T(8,128)(2,1)S(1)} %fusion.12) | copy-start | bytes 786436
  65.0 3.8 %copy-start.6 = (bf16[512,512]{1,0:T(8,128)(2,1)S(1)}, bf16[512,512]{1,0:T(8,128)(2,1)}, u32[]{:S(2)}) copy-start(bf16[512,512]{1,0:T(8,128)(2,1)} %gather_fusion) | copy-start | bytes 1572868
  65.0 3.8 %copy-start.15 = (bf16[1,512,512]{2,1,0:T(8,128)(2,1)S(1)}, bf16[1,512,512]{2,1,0:T(8,128)(2,1)}, u32[]{:S(2)}) copy-start(bf16[1,512,512]{2,1,0:T(8,128)(2,1)} %param.31) | copy-start | bytes 1572868
  71.8 89.0 %copy-start.18 = (u32[32]{0:T(128)S(1)}, u32[32]{0:T(128)}, u32[]{:S(2)}) copy-start(u32[32]{0:T(128)} %constant.80) | copy-start | bytes 388
  71.8 86.0 %all-gather.7.cloned.1.call-start = ((), (), s32[]{:S(2)}) async-start(), calls=%async_computation.3 | async-start | bytes 2621440 | tf_op jit(solution)/shard_map/all_gather | solution.py:180
  110.6 74.0 %all-gather.5.cloned.1.call-start = ((), (), s32[]{:S(2)}) async-start(), calls=%async_computation.2 | async-start | bytes 2621440 | tf_op jit(solution)/shard_map/all_gather | solution.py:186
  (2 other events, 3.5 us)
Sparse Core Ops, SparseCore 0:
  71.9 38.5 reduce-scatter.1
  112.2 45.6 all-gather.6
  160.9 21.3 all-gather.4
